TPU v7x, 256 devices: a whole 4x4x8 slice. The times are simulated.
256 devices in a mesh: row: 32 (over z_hi, y, core), col: 8 (over z_lo, x).
Axes of the slice: x: 4, y: 4, z: 8 (z_hi: 4, z_lo: 2; z = z_hi * 2 + z_lo), core: 2. Of those that a mesh axis runs over, the one named last changes fastest.
Arguments:
- known_inverse: float32 [20480, 20480], P('row', 'col'), may hold values from -1.7818667 to 1.7818667, as said below
- first_panel: float32 [20480, 512], P('col', 'row'), may hold values from -1.25 to 1.25
- second_panel: float32 [20480, 512], P('col', 'row'), may hold values from -1.25 to 1.25
- coupling: float32 [512, 512], replicated, may hold values from -0.25 to 0.25
- first_diag: float32 [512, 512], replicated, may hold values from -6 to 6
- second_diag: float32 [512, 512], replicated, may hold values from -6 to 6
- first_present: int32 [160], replicated, may hold values 0 or 1
- second_present: int32 [160], replicated, may hold values 0 or 1
Outputs:
- first_block: float32 [20480, 512], P(('row', 'col'))
- first_inverse_diag: float32 [512, 512], P(None, 'col')
- second_block: float32 [20480, 512], P(('row', 'col'))
- second_cross: float32 [512, 512], P(None, 'col')
- second_inverse_diag: float32 [512, 512], P(None, 'col')
Inputs may be any that keep to these rules, and one draw needn't show every extreme that they name: known_inverse is exactly symmetric.
All inputs are finite; a program needn't handle non-finite values.
Results may differ from a plain program's by a relative error of at most 0.000098.
Values sent between devices are 32-bit elements; how exact they have to be, the bound alone decides.
A program may use at most 64 MiB of HBM per device.

v0:
```python
import jax
import jax.numpy as jnp
from jax import lax
from jax.sharding import PartitionSpec as P

BLK = 128


def spread(block, axis, holder):
    block = jnp.where(lax.axis_index(axis) == holder, block, jnp.zeros_like(block))
    return lax.psum(block, axis)


def product(left, right):
    return jnp.dot(left, right, precision=lax.Precision.HIGHEST, preferred_element_type=jnp.float32)


def transposed(left, right):
    return lax.dot_general(
        left,
        right,
        (((0,), (0,)), ((), ())),
        precision=lax.Precision.HIGHEST,
        preferred_element_type=jnp.float32,
    )


def masked(panel, present, col_index):
    row_total, col_total = panel.shape
    blocks = row_total // BLK
    local = lax.dynamic_slice_in_dim(present, col_index * blocks, blocks)
    shaped = panel.reshape(blocks, BLK, col_total) * local.astype(jnp.float32)[:, None, None]
    return shaped.reshape(row_total, col_total)


def piece_products(known_inverse, column_one, column_two, piece_one, piece_two, coupling):
    first_block = -lax.psum_scatter(
        product(known_inverse, column_one), "col", scatter_dimension=0, tiled=True
    )
    reached = lax.psum_scatter(
        product(known_inverse, column_two), "col", scatter_dimension=0, tiled=True
    )
    first_partial = transposed(piece_one, first_block)
    second_block = -(reached + product(first_block, coupling))
    cross_partial = transposed(first_block, piece_two)
    diag_partial = transposed(piece_two, second_block)
    return (first_block, second_block, first_partial, cross_partial, diag_partial)


def on_device(
    known_inverse,
    first_panel,
    second_panel,
    coupling,
    first_diag,
    second_diag,
    first_present,
    second_present,
):
    col_count = lax.axis_size("col")
    row_index = lax.axis_index("row")
    col_index = lax.axis_index("col")
    local_one = masked(first_panel, first_present, col_index)
    local_two = masked(second_panel, second_present, col_index)
    column_one, column_two = (
        lax.all_gather(local_one, "row", axis=1, tiled=True),
        lax.all_gather(local_two, "row", axis=1, tiled=True),
    )
    band_rows = known_inverse.shape[0]
    block_cols = known_inverse.shape[1]
    piece_rows = band_rows // col_count
    width_total = coupling.shape[0]
    owner = row_index * band_rows // block_cols
    offset = row_index * band_rows % block_cols
    own_start = col_index * piece_rows
    band_one = lax.dynamic_slice_in_dim(column_one, offset, band_rows)
    band_two = lax.dynamic_slice_in_dim(column_two, offset, band_rows)
    band_one, band_two = (spread(band_one, "col", owner), spread(band_two, "col", owner))
    piece_one = lax.dynamic_slice_in_dim(band_one, own_start, piece_rows)
    piece_two = lax.dynamic_slice_in_dim(band_two, own_start, piece_rows)
    first_block, second_block, first_partial, cross_partial, diag_partial = piece_products(
        known_inverse, column_one, column_two, piece_one, piece_two, coupling
    )
    col_width = width_total // col_count
    col_start = col_index * col_width
    first_sum = lax.psum(first_partial, ("row", "col"))
    first_inverse_diag = first_diag - first_sum
    cross_sum, diag_sum = lax.psum((cross_partial, diag_partial), ("row", "col"))
    second_cross = -(cross_sum + product(first_inverse_diag, coupling))
    second_inverse_diag = second_diag - diag_sum - transposed(coupling, second_cross)
    first_out = lax.dynamic_slice_in_dim(first_inverse_diag, col_start, col_width, 1)
    cross_out = lax.dynamic_slice_in_dim(second_cross, col_start, col_width, 1)
    second_out = lax.dynamic_slice_in_dim(second_inverse_diag, col_start, col_width, 1)
    return (first_block, first_out, second_block, cross_out, second_out)


def solution(mesh):
    in_specs = (P("row", "col"), P("col", "row"), P("col", "row"), P(), P(), P(), P(), P())
    out_specs = (
        P(("row", "col"), None),
        P(None, "col"),
        P(("row", "col"), None),
        P(None, "col"),
        P(None, "col"),
    )
    return jax.shard_map(
        on_device, mesh=mesh, in_specs=in_specs, out_specs=out_specs, check_vma=False
    )
```

profile of v0, /device:TPU:2, one launch (start us, length us, event | category | flops | bytes accessed | tf_op | source)
XLA Modules:
  0.0 611.4 jit_solution(1774505497310201889)
XLA Ops:
  8.2 1.6 broadcast_multiply_fusion.1
  9.9 1.6 broadcast_multiply_fusion
  11.6 66.8 %all-gather.3.cloned.1.call-done = f32[2560,512]{0,1:T(8,128)} async-done(((f32[2560,16]{0,1:T(8,128)}), f32[2560,512]{0,1:T(8,128)}) %all-gather.3.cloned.1.call-update) | async-done | bytes 5242896 | tf_op jit(solution)/shard_map/all_gather | solution.py:66
  78.4 15.7 %convolution_bitcast_fusion.1 = f32[640,512]{0,1:T(8,128)S(1)} fusion(f32[2560,512]{0,1:T(8,128)} %all-gather.3.cloned.1.call-done, f32[640,2560]{1,0:T(8,128)} %param.8), kind=kOutput, calls=%fused_computation.1 | convolution fusion | flops 10066329600 | bytes 13107200 | tf_op jit(solution)/shard_map/dot_general | solution.py:15
  94.1 1.5 copy.27
  95.7 2.9 dynamic-slice_select_fusion.1
  98.6 45.1 %all-gather.5.cloned.1.call-done = f32[2560,512]{0,1:T(8,128)} async-done(((f32[2560,16]{0,1:T(8,128)}), f32[2560,512]{0,1:T(8,128)}) %all-gather.5.cloned.1.call-update) | async-done | bytes 5242896 | tf_op jit(solution)/shard_map/all_gather | solution.py:67
  143.7 3.0 dynamic-slice_select_fusion
  146.9 15.7 %convolution_bitcast_fusion = f32[640,512]{0,1:T(8,128)S(1)} fusion(f32[2560,512]{0,1:T(8,128)} %all-gather.5.cloned.1.call-done, f32[640,2560]{1,0:T(8,128)} %param.8), kind=kOutput, calls=%fused_computation | convolution fusion | flops 10066329600 | bytes 13107200 | tf_op jit(solution)/shard_map/dot_general | solution.py:15
  162.6 1.5 copy.29
  164.4 19.8 %reduce-scatter.7.cloned.1.call-done = f32[80,512]{1,0:T(8,128)} async-done(((f32[640,512]{1,0:T(8,128)}), f32[80,512]{1,0:T(8,128)}) %reduce-scatter.7.cloned.1.call-update) | async-done | bytes 163856
  184.2 1.0 copy.28
  185.3 92.8 %all-reduce.7.cloned.1.call-done = (f32[640,512]{0,1:T(8,128)}, f32[640,512]{0,1:T(8,128)}) async-done(((f32[640,512]{0,1:T(8,128)}, f32[640,512]{0,1:T(8,128)}), (f32[640,512]{0,1:T(8,128)}, f32[640,512]{0,1:T(8,128)})) %all-reduce.7.cloned.1.call-update) | async-done | bytes 2621456 | tf_op jit(solution)/shard_map/psum | solution.py:11
  278.0 3.1 fusion.2
  281.2 3.1 fusion.6
  284.3 37.2 %reduce-scatter.9.cloned.1.call-done = f32[80,512]{1,0:T(8,128)} async-done(((f32[640,512]{1,0:T(8,128)}), f32[80,512]{1,0:T(8,128)}) %reduce-scatter.9.cloned.1.call-update) | async-done | bytes 163856 | tf_op jit(solution)/shard_map/reduce_scatter | solution.py:40
  321.5 1.6 fusion.1
  323.2 3.2 fusion.4
  326.4 1.2 constant_dynamic-slice_fusion
  328.5 267.3 %all-reduce.5.cloned.1.call-done = (f32[512,512]{1,0:T(8,128)}, f32[512,512]{1,0:T(8,128)}, f32[512,512]{0,1:T(8,128)}) async-done(((f32[512,512]{1,0:T(8,128)}, f32[512,512]{1,0:T(8,128)}, f32[512,512]{0,1:T(8,128)}), (f32[512,512]{1,0:T(8,128)}, f32[512,512]{1,0:T(8,128)}, f32[512,512]{0,1:T(8,128)})) %all-reduce.5.cloned.1.call-update) | async-done | bytes 3145744 | tf_op jit(solution)/shard_map/psum | solution.py:86
  595.9 1.5 sub.14
  597.5 1.8 fusion
  599.5 1.8 convolution_bitcast_fusion.2
  602.9 1.6 dynamic-slice_subtract_fusion
  (30 shorter events, 4.5 us)
Async XLA Ops:
  7.2 314.3 %copy-start = (f32[512,512]{1,0:T(8,128)S(1)}, f32[512,512]{1,0:T(8,128)}, u32[]{:S(2)}) copy-start(f32[512,512]{1,0:T(8,128)} %param.11) | copy-start | bytes 3145732
  7.2 71.2 %all-gather.3.cloned.1.call-start = ((), (), s32[]{:S(2)}) async-start(), calls=%async_computation.2 | async-start | bytes 5406720 | tf_op jit(solution)/shard_map/all_gather | solution.py:66
  9.8 133.9 %all-gather.5.cloned.1.call-start = ((), (), s32[]{:S(2)}) async-start(), calls=%async_computation.3 | async-start | bytes 5406720 | tf_op jit(solution)/shard_map/all_gather | solution.py:67
  11.5 172.7 %reduce-scatter.7.cloned.1.call-start = ((), (), s32[]{:S(2)}) async-start(), calls=%async_computation.4 | async-start | bytes 1474560
  95.6 182.4 %all-reduce.7.cloned.1.call-start = ((), (), s32[]{:S(2)}) async-start(), calls=%async_computation.7 | async-start | bytes 5242880 | tf_op jit(solution)/shard_map/psum | solution.py:11
  146.7 174.8 %reduce-scatter.9.cloned.1.call-start = ((), (), s32[]{:S(2)}) async-start(), calls=%async_computation.5 | async-start | bytes 1474560 | tf_op jit(solution)/shard_map/reduce_scatter | solution.py:40
  164.1 431.7 %all-reduce.5.cloned.1.call-start = ((), (), s32[]{:S(2)}) async-start(), calls=%async_computation.6 | async-start | bytes 6291456 | tf_op jit(solution)/shard_map/psum | solution.py:86
  323.1 3.2 copy-start.3
  326.4 269.5 %copy-start.1 = (f32[512,512]{1,0:T(8,128)S(1)}, f32[512,512]{1,0:T(8,128)}, u32[]{:S(2)}) copy-start(f32[512,512]{1,0:T(8,128)} %param.12) | copy-start | bytes 3145732
  595.9 1.7 copy-start.2
Sparse Core Ops, SparseCore 0:
  11.1 67.2 all-gather.2
  81.5 62.1 all-gather.4
  146.2 37.9 reduce-scatter.6
  186.8 91.2 all-reduce.6
  280.4 41.0 reduce-scatter.8
  327.1 268.6 all-reduce.4
where the time goes:
time: 612 us; the launch traced here: 611 us
  waiting for transfers between devices  529 us (86%)
  matrix products  46.2 us (8%)
  between operations  14.3 us (2%)
  other arithmetic  13.1 us (2%)
  local copies, waits for them, and re-layouts  8.01 us (1%)
    psum x1, waiting for transfers between devices, on_device(): first_sum = lax.psum(first_partial, ('row', 'col'))  267 us
    psum x1, waiting for transfers between devices, spread(): return lax.psum(block, axis)  92.8 us
    all_gather x1, waiting for transfers between devices, on_device(): lax.all_gather(local_one, 'row', axis=1, tiled=True)  66.8 us
    all_gather x1, waiting for transfers between devices, on_device(): lax.all_gather(local_two, 'row', axis=1, tiled=True)  45.1 us
    reduce_scatter x1, waiting for transfers between devices, piece_products(): lax.psum_scatter(product(known_inverse, column_two), 'col', scatter_dimen...  37.2 us
    dot_general x4, matrix products, product(): jnp.dot(left, right, precision=lax.Precision.HIGHEST, preferred_element_t...  35 us
    unnamed x7, waiting for transfers between devices  19.9 us
  transfers between devices with their start and end apart: 6, of which 6 were waited for; matrix products, arithmetic and copies ran while one was open for 8% of the time, Pallas kernels for 0%

commit v1 on v0

--- a/solution.py
+++ b/solution.py
@@ -83,7 +83,8 @@
     )
     col_width = width_total // col_count
     col_start = col_index * col_width
-    first_sum = lax.psum(first_partial, ("row", "col"))
+    match_the_rows = lambda view: lax.psum(lax.psum(view, "row"), "col")
+    first_sum = match_the_rows(first_partial)
     first_inverse_diag = first_diag - first_sum
     cross_sum, diag_sum = lax.psum((cross_partial, diag_partial), ("row", "col"))
     second_cross = -(cross_sum + product(first_inverse_diag, coupling))

time: 612 us -> 999 us (1.63)
  waiting for transfers between devices: 529 us -> 915 us
    psum x1 -> x3, waiting for transfers between devices: 267 us -> 621 us  [the longest x2 360 us: on_device(): match_the_rows = lambda view: lax.psum(lax.psum(view, 'row'), 'col')]
    all_gather x1, waiting for transfers between devices: 45.1 us -> 65.3 us  [on_device(): lax.all_gather(local_two, 'row', axis=1, tiled=True)]
    unnamed x7 -> x9, waiting for transfers between devices: 19.9 us -> 33.5 us
  transfers between devices with their start and end apart: 6 -> 8, of which waited for: 6 -> 8; matrix products, arithmetic and copies ran while one was open for 8% -> 3% of each run, Pallas kernels for 0% -> 0%
where the time goes in v1:
time: 999 us; the launch traced here: 998 us
  waiting for transfers between devices  915 us (92%)
  matrix products  47.3 us (5%)
  between operations  14.3 us (1%)
  other arithmetic  12.1 us (1%)
    psum x2, waiting for transfers between devices, on_device(): match_the_rows = lambda view: lax.psum(lax.psum(view, 'row'), 'col')  360 us
    psum x1, waiting for transfers between devices, on_device(): lax.psum((cross_partial, diag_partial), ('row', 'col'))  261 us
    psum x1, waiting for transfers between devices, spread(): return lax.psum(block, axis)  85.1 us
    all_gather x1, waiting for transfers between devices, on_device(): lax.all_gather(local_one, 'row', axis=1, tiled=True)  68.5 us
    all_gather x1, waiting for transfers between devices, on_device(): lax.all_gather(local_two, 'row', axis=1, tiled=True)  65.3 us
    reduce_scatter x1, waiting for transfers between devices, piece_products(): lax.psum_scatter(product(known_inverse, column_two), 'col', scatter_dimen...  41.8 us
    dot_general x4, matrix products, product(): jnp.dot(left, right, precision=lax.Precision.HIGHEST, preferred_element_t...  36.2 us
    unnamed x9, waiting for transfers between devices  33.5 us
  transfers between devices with their start and end apart: 8, of which 8 were waited for; matrix products, arithmetic and copies ran while one was open for 3% of the time, Pallas kernels for 0%

profile of v1, /device:TPU:2, one launch (start us, length us, event | category | flops | bytes accessed | tf_op | source)
XLA Modules:
  0.0 998.1 jit_solution(1562031844266467298)
XLA Ops:
  8.2 1.6 broadcast_multiply_fusion.1
  9.8 68.5 %all-gather.3.cloned.1.call-done = f32[2560,512]{0,1:T(8,128)} async-done(((f32[2560,16]{0,1:T(8,128)}), f32[2560,512]{0,1:T(8,128)}) %all-gather.3.cloned.1.call-update) | async-done | bytes 5242896 | tf_op jit(solution)/shard_map/all_gather | solution.py:66
  78.4 15.7 %convolution_bitcast_fusion.1 = f32[640,512]{0,1:T(8,128)S(1)} fusion(f32[2560,512]{0,1:T(8,128)} %all-gather.3.cloned.1.call-done, f32[640,2560]{1,0:T(8,128)} %param.8), kind=kOutput, calls=%fused_computation.1 | convolution fusion | flops 10066329600 | bytes 13107200 | tf_op jit(solution)/shard_map/dot_general | solution.py:15
  94.1 1.5 copy.27
  95.7 3.0 dynamic-slice_select_fusion.1
  100.3 33.4 %reduce-scatter.7.cloned.1.call-done = f32[80,512]{1,0:T(8,128)} async-done(((f32[640,512]{1,0:T(8,128)}), f32[80,512]{1,0:T(8,128)}) %reduce-scatter.7.cloned.1.call-update) | async-done | bytes 163856
  134.7 85.1 %all-reduce.7.cloned.1.call-done = f32[640,512]{0,1:T(8,128)} async-done(((f32[640,512]{0,1:T(8,128)}), f32[640,512]{0,1:T(8,128)}) %all-reduce.7.cloned.1.call-update) | async-done | bytes 1310736 | tf_op jit(solution)/shard_map/psum | solution.py:11
  219.8 3.0 fusion.2
  223.1 65.3 %all-gather.5.cloned.1.call-done = f32[2560,512]{0,1:T(8,128)} async-done(((f32[2560,16]{0,1:T(8,128)}), f32[2560,512]{0,1:T(8,128)}) %all-gather.5.cloned.1.call-update) | async-done | bytes 5242896 | tf_op jit(solution)/shard_map/all_gather | solution.py:67
  288.4 15.7 %convolution_bitcast_fusion = f32[640,512]{0,1:T(8,128)S(1)} fusion(f32[2560,512]{0,1:T(8,128)} %all-gather.5.cloned.1.call-done, f32[640,2560]{1,0:T(8,128)} %param.8), kind=kOutput, calls=%fused_computation | convolution fusion | flops 10066329600 | bytes 13107200 | tf_op jit(solution)/shard_map/dot_general | solution.py:15
  304.2 1.5 copy.29
  305.7 2.9 dynamic-slice_select_fusion
  308.6 269.4 %all-reduce.9.cloned.1.call-done = f32[512,512]{1,0:T(8,128)} async-done(((f32[512,512]{1,0:T(8,128)}), f32[512,512]{1,0:T(8,128)}) %all-reduce.9.cloned.1.call-update) | async-done | bytes 1048592 | tf_op jit(solution)/shard_map/psum | solution.py:86
  578.4 41.8 %reduce-scatter.9.cloned.1.call-done = f32[80,512]{1,0:T(8,128)} async-done(((f32[640,512]{1,0:T(8,128)}), f32[80,512]{1,0:T(8,128)}) %reduce-scatter.9.cloned.1.call-update) | async-done | bytes 163856 | tf_op jit(solution)/shard_map/reduce_scatter | solution.py:40
  620.2 1.6 fusion.1
  621.8 90.3 %all-reduce.13.cloned.1.call-done = (f32[512,512]{1,0:T(8,128)}, f32[640,512]{0,1:T(8,128)}) async-done(((f32[512,512]{1,0:T(8,128)}, f32[640,512]{0,1:T(8,128)}), (f32[512,512]{1,0:T(8,128)}, f32[640,512]{0,1:T(8,128)})) %all-reduce.13.cloned.1.call-update) | async-done | bytes 2359312 | tf_op jit(solution)/shard_map/psum | solution.py:86
  712.1 3.1 fusion.6
  715.2 3.1 fusion.4
  718.4 1.2 constant_dynamic-slice_fusion
  720.5 1.4 sub.14
  722.9 261.0 %all-reduce.11.cloned.1.call-done = (f32[512,512]{1,0:T(8,128)}, f32[512,512]{0,1:T(8,128)}) async-done(((f32[512,512]{1,0:T(8,128)}, f32[512,512]{0,1:T(8,128)}), (f32[512,512]{1,0:T(8,128)}, f32[512,512]{0,1:T(8,128)})) %all-reduce.11.cloned.1.call-update) | async-done | bytes 2097168 | tf_op jit(solution)/shard_map/psum | solution.py:89
  983.8 3.1 fusion
  986.9 1.8 convolution_bitcast_fusion.2
  989.7 1.6 dynamic-slice_subtract_fusion
  (36 shorter events, 7.1 us)
Async XLA Ops:
  7.2 613.0 %copy-start = (f32[512,512]{1,0:T(8,128)S(1)}, f32[512,512]{1,0:T(8,128)}, u32[]{:S(2)}) copy-start(f32[512,512]{1,0:T(8,128)} %param.11) | copy-start | bytes 3145732
  7.2 71.2 %all-gather.3.cloned.1.call-start = ((), (), s32[]{:S(2)}) async-start(), calls=%async_computation.2 | async-start | bytes 5406720 | tf_op jit(solution)/shard_map/all_gather | solution.py:66
  9.8 123.9 %reduce-scatter.7.cloned.1.call-start = ((), (), s32[]{:S(2)}) async-start(), calls=%async_computation.6 | async-start | bytes 1474560
  95.6 124.2 %all-reduce.7.cloned.1.call-start = ((), (), s32[]{:S(2)}) async-start(), calls=%async_computation.3 | async-start | bytes 2621440 | tf_op jit(solution)/shard_map/psum | solution.py:11
  98.7 0.9 copy-start.3
  98.7 189.7 %all-gather.5.cloned.1.call-start = ((), (), s32[]{:S(2)}) async-start(), calls=%async_computation.5 | async-start | bytes 5406720 | tf_op jit(solution)/shard_map/all_gather | solution.py:67
  100.3 477.8 %all-reduce.9.cloned.1.call-start = ((), (), s32[]{:S(2)}) async-start(), calls=%async_computation.4 | async-start | bytes 2097152 | tf_op jit(solution)/shard_map/psum | solution.py:86
  222.9 397.3 %reduce-scatter.9.cloned.1.call-start = ((), (), s32[]{:S(2)}) async-start(), calls=%async_computation.7 | async-start | bytes 1474560 | tf_op jit(solution)/shard_map/reduce_scatter | solution.py:40
  305.7 406.5 %all-reduce.13.cloned.1.call-start = ((), (), s32[]{:S(2)}) async-start(), calls=%async_computation.9 | async-start | bytes 4718592 | tf_op jit(solution)/shard_map/psum | solution.py:86
  578.1 405.7 %all-reduce.11.cloned.1.call-start = ((), (), s32[]{:S(2)}) async-start(), calls=%async_computation.8 | async-start | bytes 4194304 | tf_op jit(solution)/shard_map/psum | solution.py:89
  621.8 96.6 %copy-start.2 = (f32[80,512]{1,0:T(8,128)}, f32[80,512]{1,0:T(8,128)S(1)}, u32[]{:S(2)}) copy-start(f32[80,512]{1,0:T(8,128)S(1)} %fusion.1) | copy-start | bytes 491524
  718.4 2.1 copy-start.1
Sparse Core Ops, SparseCore 0:
  11.1 67.2 all-gather.2
  95.7 37.9 reduce-scatter.6
  136.4 83.4 all-reduce.6
  222.8 65.6 all-gather.4
  290.9 287.1 all-reduce.8
  580.5 39.6 reduce-scatter.8
  622.9 89.1 all-reduce.12
  718.5 265.2 all-reduce.10
